TPU v7x, 512 devices: a whole 4x8x8 slice. The times are simulated.
512 devices in a mesh: grp: 16 (over y, core), mdl: 32 (over x, z).
Axes of the slice: x: 4, y: 8, z: 8, core: 2. Of those that a mesh axis runs over, the one named last changes fastest.
Arguments:
- row_states: bfloat16 [6144, 1024], P('grp', 'mdl'), may hold values from -6 to 6
- ffn_gain: bfloat16 [1024], replicated, may hold values from 0.25 to 1.75
- ffn_in: bfloat16 [1024, 32768], P('grp', 'mdl'), may hold values from -0.1875 to 0.1875
- ffn_out: bfloat16 [32768, 1024], P('mdl', 'grp'), may hold values from -0.0625 to 0.0625
- final_gain: bfloat16 [1024], replicated, may hold values from 0.25 to 1.75
- kv_weight: bfloat16 [2, 1024, 16384], P(None, None, 'mdl'), may hold values from -0.1875 to 0.1875
- queries: bfloat16 [4096, 16384], P('grp', 'mdl'), may hold values from -36 to 36
- attn_out: bfloat16 [16384, 1024], P('mdl'), may hold values from -0.75 to 0.75
- row_question: int32 [6144], replicated, may hold values from 0 to 15, as said below
Outputs:
- cross_out: bfloat16 [4096, 1024], P(('grp', 'mdl'))
Inputs may be any that keep to these rules, and one draw needn't show every extreme that they name: `row_question`: within each block of 384 rows (one row group) the rows are sorted by question; in every block each question owns a multiple of 8 rows, at least 8 and at most 72, and one question, drawn from the seed, owns exactly 72 rows of every block.
All inputs are finite; a program needn't handle non-finite values.
Results may differ from a plain program's by a relative error of at most 0.029.
Values may be sent and summed in bfloat16 or wider, within the bound.
No kernel may reach another device: no remote copies, remote signals or barrier semaphores. Data moves between devices by JAX's collectives and lax.ppermute only.
A program may use at most 64 MiB of HBM per device.

v0:
```python
import jax
import jax.numpy as jnp
from jax import lax
from jax.sharding import PartitionSpec as P

HEAD_DIM = 128


def rms_normalize(states, gain):
    wide = states.astype(jnp.float32)
    factor = lax.rsqrt(jnp.mean(wide * wide, axis=-1, keepdims=True) + 1e-06)
    return (wide * factor * gain.astype(jnp.float32)).astype(jnp.bfloat16)


def bucket_plan(row_question, rows_local, groups, my_group):
    capacity = 3 * rows_local // groups
    owners = row_question.reshape(groups, rows_local)
    owner_table = (owners[:, :, None] == jnp.arange(groups, dtype=jnp.int32)[None, None, :]).astype(
        jnp.int32
    )
    counts = jnp.sum(owner_table, axis=1)
    starts = jnp.cumsum(counts, axis=1) - counts
    slot_index = jnp.arange(capacity, dtype=jnp.int32)
    sent_counts = lax.dynamic_index_in_dim(counts, my_group, 0, keepdims=False)
    sent_starts = lax.dynamic_index_in_dim(starts, my_group, 0, keepdims=False)
    send_valid = slot_index[None, :] < sent_counts[:, None]
    send_rows = jnp.minimum(sent_starts[:, None] + slot_index[None, :], rows_local - 1)
    got_counts = lax.dynamic_index_in_dim(counts, my_group, 1, keepdims=False)
    got_valid = (slot_index[None, :] < got_counts[:, None]).reshape(-1)
    return (capacity, send_rows, send_valid, got_valid)


def pack_slots(source, send_rows, send_valid):
    picked = jnp.take(source, send_rows.reshape(-1), axis=0)
    picked = picked.reshape(send_rows.shape[0], send_rows.shape[1], source.shape[1])
    picked = jnp.where(send_valid[:, :, None], picked, jnp.zeros((), source.dtype))
    return picked.reshape(send_rows.shape[0], -1)


def local(
    row_states, ffn_gain, ffn_in, ffn_out, final_gain, kv_weight, queries, attn_out, row_question
):
    groups = lax.axis_size("grp")
    my_group = lax.axis_index("grp")
    rows_local = row_states.shape[0]
    full_rows = lax.all_gather(row_states, "mdl", axis=1, tiled=True)
    normed = rms_normalize(full_rows, ffn_gain)
    pre_active = jnp.dot(
        normed,
        lax.all_gather(ffn_in, "grp", axis=0, tiled=True),
        preferred_element_type=jnp.float32,
    )
    hidden = jnp.maximum(pre_active, 0.0).astype(jnp.bfloat16)
    ffn_terms = jnp.dot(
        hidden,
        lax.all_gather(ffn_out, "grp", axis=1, tiled=True),
        preferred_element_type=jnp.float32,
    )
    ffn_sum = lax.psum_scatter(ffn_terms, "mdl", scatter_dimension=1, tiled=True)
    enc_state = (row_states.astype(jnp.float32) + ffn_sum).astype(jnp.bfloat16)
    capacity, send_rows, send_valid, got_valid = bucket_plan(
        row_question, rows_local, groups, my_group
    )
    head_cols = kv_weight.shape[2]
    outgoing = pack_slots(enc_state, send_rows, send_valid)
    arrived = lax.all_to_all(outgoing, "grp", split_axis=0, concat_axis=0, tiled=True)
    slot_rows = lax.all_gather(arrived.reshape(groups * capacity, -1), "mdl", axis=1, tiled=True)
    encoded = rms_normalize(slot_rows, final_gain)
    projected = jnp.einsum(
        "rd,kdc->krc", encoded, kv_weight, preferred_element_type=jnp.float32
    ).astype(jnp.bfloat16)
    key_rows = projected[0]
    value_rows = projected[1]
    targets = queries.shape[0]
    heads_local = head_cols // HEAD_DIM
    query_heads = queries.reshape(targets, heads_local, HEAD_DIM)
    key_heads = key_rows.reshape(-1, heads_local, HEAD_DIM)
    value_heads = value_rows.reshape(-1, heads_local, HEAD_DIM)
    scores = jnp.einsum("thd,rhd->htr", query_heads, key_heads, preferred_element_type=jnp.float32)
    slot_mask = got_valid[None, None, :]
    scores = jnp.where(slot_mask, scores, -1e30)
    top_score = jnp.max(scores, axis=-1, keepdims=True)
    raised = jnp.where(slot_mask, jnp.exp(scores - top_score), 0.0)
    probabilities = (raised / jnp.sum(raised, axis=-1, keepdims=True)).astype(jnp.bfloat16)
    attended = jnp.einsum(
        "htr,rhd->thd", probabilities, value_heads, preferred_element_type=jnp.float32
    )
    attended = attended.astype(jnp.bfloat16).reshape(targets, head_cols)
    return lax.psum_scatter(
        jnp.dot(attended, attn_out, preferred_element_type=jnp.float32).astype(jnp.bfloat16),
        "mdl",
        scatter_dimension=0,
        tiled=True,
    )


def solution(mesh):
    in_specs = (
        P("grp", "mdl"),
        P(),
        P("grp", "mdl"),
        P("mdl", "grp"),
        P(),
        P(None, None, "mdl"),
        P("grp", "mdl"),
        P("mdl", None),
        P(),
    )
    out_specs = P(("grp", "mdl"), None)
    return jax.shard_map(local, mesh=mesh, in_specs=in_specs, out_specs=out_specs, check_vma=False)
```

profile of v0, /device:TPU:8, one launch (start us, length us, event | category | flops | bytes accessed | tf_op | source)
XLA Modules:
  0.0 669.9 jit_solution(2616351746955564816)
XLA Ops:
  6.5 0.7 all-gather.4.cloned.1.call-update
  7.3 0.7 all-gather.6.cloned.1.call-update
  8.1 0.7 convert_element_type.51
  8.7 56.0 %all_gather.12 = bf16[384,1024]{0,1:T(8,128)(2,1)S(1)} all-gather(bf16[384,32]{0,1:T(8,128)(2,1)} %param.9), channel_id=1, replica_groups=mesh['grp'=16,'mdl'=32] {'mdl'}, dimensions={1}, use_global_device_ids=true | all-gather | bytes 811008 | tf_op jit(solution)/shard_map/all_gather | solution.py:46
  64.7 0.2 fusion.14
  65.0 33.6 %all-gather.6.cloned.1.call-done = bf16[1024,1024]{0,1:T(8,128)(2,1)} async-done(((bf16[1024,64]{0,1:T(8,128)(2,1)}), bf16[1024,1024]{0,1:T(8,128)(2,1)}) %all-gather.6.cloned.1.call-update) | async-done | bytes 2097168 | tf_op jit(solution)/shard_map/all_gather | solution.py:56
  98.5 5.6 fusion.22
  104.2 0.4 convert_reduce_fusion
  104.6 0.2 reduce_window_sum.11
  105.0 0.2 broadcast_in_dim.60
  105.2 0.2 broadcast_in_dim.61
  105.5 0.2 broadcast_in_dim.62
  105.7 0.2 broadcast_in_dim.63
  106.0 222.1 %reduce-scatter.3.cloned.1.call-done = f32[384,32]{0,1:T(8,128)} async-done(((f32[384,1024]{0,1:T(8,128)}), f32[384,32]{0,1:T(8,128)}) %reduce-scatter.3.cloned.1.call-update) | async-done | bytes 49168 | tf_op jit(solution)/shard_map/reduce_scatter | solution.py:59
  328.1 0.8 add_convert_fusion
  329.0 2.9 gather_fusion
  332.0 0.2 gather.7
  332.2 0.5 broadcast.116
  332.7 0.7 reduce.5
  333.4 13.6 %all_to_all.6 = bf16[16,2,1152]{2,1,0:T(2,128)(2,1)S(1)} all-to-all(bf16[16,2,1152]{2,1,0:T(2,128)(2,1)S(1)} %reshape.169), channel_id=1, replica_groups=mesh['grp'=16,'mdl'=32] {'grp'}, dimensions={0} | all-to-all | bytes 147456 | tf_op jit(solution)/shard_map/all_to_all | solution.py:66
  347.0 0.4 reduce.1
  347.5 0.2 reshape.154
  347.7 0.8 copy.30
  348.6 0.2 dynamic-slice_reduce_fusion
  348.9 78.2 %all-gather.8.cloned.1.call-done = bf16[1152,1024]{0,1:T(8,128)(2,1)} async-done(((bf16[1152,32]{0,1:T(8,128)(2,1)}), bf16[1152,1024]{0,1:T(8,128)(2,1)}) %all-gather.8.cloned.1.call-update) | async-done | bytes 2359312 | tf_op jit(solution)/shard_map/all_gather | solution.py:67
  427.1 2.3 fusion.2
  429.5 3.5 fusion.8
  432.9 1.2 fusion.40
  434.2 5.5 fusion.41
  439.7 2.9 fusion.17
  442.6 1.3 convolution_convert_fusion.1
  443.9 219.4 %reduce-scatter.5.cloned.1.call-done = bf16[8,1024]{1,0:T(8,128)(2,1)} async-done(((bf16[256,1024]{1,0:T(8,128)(2,1)}), bf16[8,1024]{1,0:T(8,128)(2,1)}) %reduce-scatter.5.cloned.1.call-update) | async-done | bytes 16400 | tf_op jit(solution)/shard_map/reduce_scatter | solution.py:89
  (39 shorter events, 1.0 us)
Async XLA Ops:
  6.5 422.9 %copy-start = (bf16[2,1024,512]{2,1,0:T(8,128)(2,1)S(1)}, bf16[2,1024,512]{2,1,0:T(8,128)(2,1)}, u32[]{:S(2)}) copy-start(bf16[2,1024,512]{2,1,0:T(8,128)(2,1)} %param.14) | copy-start | bytes 6291460
  6.5 58.4 %all-gather.4.cloned.1.call-start = ((), (), s32[]{:S(2)}) async-start(), calls=%async_computation.3 | async-start | bytes 2228224 | tf_op jit(solution)/shard_map/all_gather | solution.py:50
  7.3 91.3 %all-gather.6.cloned.1.call-start = ((), (), s32[]{:S(2)}) async-start(), calls=%async_computation.4 | async-start | bytes 2228224 | tf_op jit(solution)/shard_map/all_gather | solution.py:56
  8.0 320.1 %reduce-scatter.3.cloned.1.call-start = ((), (), s32[]{:S(2)}) async-start(), calls=%async_computation.5 | async-start | bytes 1622016 | tf_op jit(solution)/shard_map/reduce_scatter | solution.py:59
  64.9 39.3 %copy-start.4 = (s32[6144]{0:T(1024)S(1)}, s32[6144]{0:T(1024)}, u32[]{:S(2)}) copy-start(s32[6144]{0:T(1024)} %param.17) | copy-start | bytes 73732
  104.1 224.0 %copy-start.3 = (bf16[384,32]{0,1:T(8,128)(2,1)S(1)}, bf16[384,32]{0,1:T(8,128)(2,1)}, u32[]{:S(2)}) copy-start(bf16[384,32]{0,1:T(8,128)(2,1)} %param.9) | copy-start | bytes 73732
  104.1 322.9 %all-gather.8.cloned.1.call-start = ((), (), s32[]{:S(2)}) async-start(), calls=%async_computation.6 | async-start | bytes 2433024 | tf_op jit(solution)/shard_map/all_gather | solution.py:67
  329.0 19.5 %copy-start.5 = (bf16[1024]{0:T(1024)(128)(2,1)S(1)}, bf16[1024]{0:T(1024)(128)(2,1)}, u32[]{:S(2)}) copy-start(bf16[1024]{0:T(1024)(128)(2,1)} %param.13) | copy-start | bytes 6148
  348.5 314.8 %reduce-scatter.5.cloned.1.call-start = ((), (), s32[]{:S(2)}) async-start(), calls=%async_computation.7 | async-start | bytes 540672 | tf_op jit(solution)/shard_map/reduce_scatter | solution.py:89
  427.1 2.4 copy-start.1
  432.9 1.2 copy-start.6
  439.7 3.0 copy-start.2
Sparse Core Ops, SparseCore 0:
  9.5 46.1 all-gather.3
  57.7 40.7 all-gather.5
  104.3 223.7 reduce-scatter.2
  348.6 78.4 all-gather.7
  444.0 219.2 reduce-scatter.4
where the time goes:
time: 670 us
  waiting for transfers between devices  555 us (83%)
  blocking collectives  69.5 us (10%)
  matrix products  18.7 us (3%)
  between operations  13.3 us (2%)
  local copies, waits for them, and re-layouts  7.41 us (1%)
    reduce_scatter x1, waiting for transfers between devices, local(): lax.psum_scatter(ffn_terms, 'mdl', scatter_dimension=1, tiled=True)  222 us
    reduce_scatter x1, waiting for transfers between devices, local(): lax.psum_scatter(jnp.dot(attended, attn_out, preferred_element_type=jnp.f...  219 us
    all_gather x1, waiting for transfers between devices, local(): lax.all_gather(arrived.reshape(groups * capacity, -1), 'mdl', axis=1, til...  78.2 us
    all_gather x1, blocking collectives, local(): full_rows = lax.all_gather(row_states, 'mdl', axis=1, tiled=True)  56 us
    all_gather x1, waiting for transfers between devices, local(): lax.all_gather(ffn_out, 'grp', axis=1, tiled=True)  33.6 us
    all_to_all x1, blocking collectives, local(): lax.all_to_all(outgoing, 'grp', split_axis=0, concat_axis=0, tiled=True)  13.6 us
  transfers between devices with their start and end apart: 5, of which 4 were waited for; matrix products, arithmetic and copies ran while one was open for 0% of the time, Pallas kernels for 0%

commit v1 on v0

--- a/solution.py
+++ b/solution.py
@@ -4,6 +4,24 @@
 from jax.sharding import PartitionSpec as P
 
 HEAD_DIM = 128
+
+
+def collect(value, axis, dim):
+    ways, here, lap = (lax.axis_size(axis), lax.axis_index(axis), value.shape[dim])
+    lengths = [n * ways if d == dim else n for d, n in enumerate(value.shape)]
+    full = lax.dynamic_update_slice_in_dim(
+        jnp.zeros(lengths, value.dtype), value, here * lap, axis=dim
+    )
+    going_up = going_down = value
+    for far in range(1, ways // 2 + 1):
+        going_up = lax.ppermute(going_up, axis, [(d, (d + 1) % ways) for d in range(ways)])
+        full = lax.dynamic_update_slice_in_dim(full, going_up, (here - far) % ways * lap, axis=dim)
+        if 2 * far < ways:
+            going_down = lax.ppermute(going_down, axis, [(d, (d - 1) % ways) for d in range(ways)])
+            full = lax.dynamic_update_slice_in_dim(
+                full, going_down, (here + far) % ways * lap, axis=dim
+            )
+    return full
 
 
 def rms_normalize(states, gain):
@@ -51,11 +69,7 @@
         preferred_element_type=jnp.float32,
     )
     hidden = jnp.maximum(pre_active, 0.0).astype(jnp.bfloat16)
-    ffn_terms = jnp.dot(
-        hidden,
-        lax.all_gather(ffn_out, "grp", axis=1, tiled=True),
-        preferred_element_type=jnp.float32,
-    )
+    ffn_terms = jnp.dot(hidden, collect(ffn_out, "grp", 1), preferred_element_type=jnp.float32)
     ffn_sum = lax.psum_scatter(ffn_terms, "mdl", scatter_dimension=1, tiled=True)
     enc_state = (row_states.astype(jnp.float32) + ffn_sum).astype(jnp.bfloat16)
     capacity, send_rows, send_valid, got_valid = bucket_plan(

time: 670 us -> 679 us (1.013)
  waiting for transfers between devices: 555 us -> 536 us
  starting transfers between devices: 0.16 us -> 14.8 us
  local copies, waits for them, and re-layouts: 7.41 us -> 19.9 us
    all_gather x1 -> x0, waiting for transfers between devices: 33.6 us -> none  [local(): lax.all_gather(ffn_out, 'grp', axis=1, tiled=True)]
    ppermute x0 -> x15, starting transfers between devices: none -> 14.5 us  [the longest x7 14.4 us: collect(): lax.ppermute(going_down, axis, [(d, (d - 1) % ways) for d in range(ways)])]
    ppermute x0 -> x15, waiting for transfers between devices: none -> 11.8 us  [the longest x8 11.3 us: collect(): lax.ppermute(going_up, axis, [(d, (d + 1) % ways) for d in range(ways)])]
    dynamic_update_slice x0 -> x16, local copies, waits for them, and re-layouts: none -> 10.6 us  [the longest x8 5.28 us: collect(): lax.dynamic_update_slice_in_dim(full, going_up, (here - far) % ways * lap...]
  transfers between devices with their start and end apart: 5 -> 19, of which waited for: 4 -> 13; matrix products, arithmetic and copies ran while one was open for 0% -> 2% of each run, Pallas kernels for 0% -> 0%
where the time goes in v1:
time: 679 us
  waiting for transfers between devices  536 us (79%)
  blocking collectives  69.6 us (10%)
  local copies, waits for them, and re-layouts  19.9 us (3%)
  matrix products  19.1 us (3%)
  starting transfers between devices  14.8 us (2%)
  between operations  13.7 us (2%)
    reduce_scatter x1, waiting for transfers between devices, local(): lax.psum_scatter(ffn_terms, 'mdl', scatter_dimension=1, tiled=True)  226 us
    reduce_scatter x1, waiting for transfers between devices, local(): lax.psum_scatter(jnp.dot(attended, attn_out, preferred_element_type=jnp.f...  220 us
    all_gather x1, waiting for transfers between devices, local(): lax.all_gather(arrived.reshape(groups * capacity, -1), 'mdl', axis=1, til...  78 us
    all_gather x1, blocking collectives, local(): full_rows = lax.all_gather(row_states, 'mdl', axis=1, tiled=True)  56 us
    ppermute x7, starting transfers between devices, collect(): lax.ppermute(going_down, axis, [(d, (d - 1) % ways) for d in range(ways)])  14.4 us
    all_to_all x1, blocking collectives, local(): lax.all_to_all(outgoing, 'grp', split_axis=0, concat_axis=0, tiled=True)  13.6 us
  transfers between devices with their start and end apart: 19, of which 13 were waited for; matrix products, arithmetic and copies ran while one was open for 2% of the time, Pallas kernels for 0%

profile of v1, /device:TPU:8, one launch (start us, length us, event | category | flops | bytes accessed | tf_op | source)
XLA Modules:
  0.0 678.8 jit_solution(4967779151182035948)
XLA Ops:
  6.5 0.7 all-gather.3.cloned.1.call-update
  7.3 1.7 collective-permute-start.1
  9.1 56.0 %all_gather.9 = bf16[384,1024]{0,1:T(8,128)(2,1)S(1)} all-gather(bf16[384,32]{0,1:T(8,128)(2,1)} %param.9), channel_id=1, replica_groups=mesh['grp'=16,'mdl'=32] {'mdl'}, dimensions={1}, use_global_device_ids=true | all-gather | bytes 811008 | tf_op jit(solution)/shard_map/all_gather | solution.py:64
  65.6 1.6 broadcast_in_dim.67
  67.9 1.7 collective-permute-start.3
  70.9 1.3 collective-permute-done.2
  72.3 2.0 collective-permute-start.5
  75.6 1.0 collective-permute-done.4
  76.8 1.9 collective-permute-start.7
  80.0 1.0 collective-permute-done.6
  81.2 1.9 collective-permute-start.9
  83.1 0.7 constant_dynamic-update-slice_fusion.8
  84.4 1.0 collective-permute-done.8
  85.6 2.2 collective-permute-start.11
  89.1 1.3 collective-permute-done.10
  90.4 3.0 collective-permute-start.13
  94.8 1.3 collective-permute-done.12
  97.4 4.3 collective-permute-done.14
  102.3 5.6 fusion.22
  109.8 226.2 %reduce-scatter.3.cloned.1.call-done = f32[384,32]{0,1:T(8,128)} async-done(((f32[384,1024]{0,1:T(8,128)}), f32[384,32]{0,1:T(8,128)}) %reduce-scatter.3.cloned.1.call-update) | async-done | bytes 49168 | tf_op jit(solution)/shard_map/reduce_scatter | solution.py:73
  336.0 0.8 add_convert_fusion
  336.9 2.9 gather_fusion
  341.3 13.6 %all_to_all.6 = bf16[16,2,1152]{2,1,0:T(2,128)(2,1)S(1)} all-to-all(bf16[16,2,1152]{2,1,0:T(2,128)(2,1)S(1)} %reshape.169), channel_id=1, replica_groups=mesh['grp'=16,'mdl'=32] {'grp'}, dimensions={0} | all-to-all | bytes 147456 | tf_op jit(solution)/shard_map/all_to_all | solution.py:80
  355.6 0.8 copy.30
  357.0 78.0 %all-gather.5.cloned.1.call-done = bf16[1152,1024]{0,1:T(8,128)(2,1)} async-done(((bf16[1152,32]{0,1:T(8,128)(2,1)}), bf16[1152,1024]{0,1:T(8,128)(2,1)}) %all-gather.5.cloned.1.call-update) | async-done | bytes 2359312 | tf_op jit(solution)/shard_map/all_gather | solution.py:81
  435.0 2.3 fusion.2
  437.4 3.5 fusion.8
  440.9 1.6 fusion.40
  442.5 5.5 fusion.41
  448.0 3.3 fusion.17
  451.3 1.3 convolution_convert_fusion.1
  452.6 219.6 %reduce-scatter.5.cloned.1.call-done = bf16[8,1024]{1,0:T(8,128)(2,1)} async-done(((bf16[256,1024]{1,0:T(8,128)(2,1)}), bf16[8,1024]{1,0:T(8,128)(2,1)}) %reduce-scatter.5.cloned.1.call-update) | async-done | bytes 16400 | tf_op jit(solution)/shard_map/reduce_scatter | solution.py:103
  (87 shorter events, 15.4 us)
Async XLA Ops:
  6.5 430.9 %copy-start = (bf16[2,1024,512]{2,1,0:T(8,128)(2,1)S(1)}, bf16[2,1024,512]{2,1,0:T(8,128)(2,1)}, u32[]{:S(2)}) copy-start(bf16[2,1024,512]{2,1,0:T(8,128)(2,1)} %param.14) | copy-start | bytes 6291460
  6.5 59.0 %copy-start.6 = (bf16[1024]{0:T(1024)(128)(2,1)S(1)}, bf16[1024]{0:T(1024)(128)(2,1)}, u32[]{:S(2)}) copy-start(bf16[1024]{0:T(1024)(128)(2,1)} %param.10) | copy-start | bytes 6148
  6.5 95.8 %all-gather.3.cloned.1.call-start = ((), (), s32[]{:S(2)}) async-start(), calls=%async_computation.3 | async-start | bytes 2228224 | tf_op jit(solution)/shard_map/all_gather | solution.py:68
  7.3 60.0 %copy-start.3 = (bf16[1024,64]{0,1:T(8,128)(2,1)S(1)}, bf16[1024,64]{0,1:T(8,128)(2,1)}, u32[]{:S(2)}) copy-start(bf16[1024,64]{0,1:T(8,128)(2,1)} %param.12) | copy-start | bytes 393220
  7.3 328.7 %reduce-scatter.3.cloned.1.call-start = ((), (), s32[]{:S(2)}) async-start(), calls=%async_computation.4 | async-start | bytes 1622016 | tf_op jit(solution)/shard_map/reduce_scatter | solution.py:73
  7.3 60.6 %collective-permute-start = (bf16[1024,64]{0,1:T(8,128)(2,1)}, bf16[1024,64]{0,1:T(8,128)(2,1)S(1)}, u32[]{:S(2)}, u32[]{:S(2)}) collective-permute-start(bf16[1024,64]{0,1:T(8,128)(2,1)} %param.12), channel_id=1, source_target_pairs={{0,32},{32,64},{64,96},{96,128},{128,160},{160,192},{192,224},{224... | collective-permute-start | bytes 393224 | tf_op jit(solution)/shard_map/ppermute | solution.py:17
  7.3 60.5 %collective-permute-start.1 = (bf16[1024,64]{0,1:T(8,128)(2,1)}, bf16[1024,64]{0,1:T(8,128)(2,1)S(1)}, u32[]{:S(2)}, u32[]{:S(2)}) collective-permute-start(bf16[1024,64]{0,1:T(8,128)(2,1)} %param.12), channel_id=1, source_target_pairs={{0,480},{32,0},{64,32},{96,64},{128,96},{160,128},{192,160},{224,1... | collective-permute-start | bytes 393224 | tf_op jit(solution)/shard_map/ppermute | solution.py:20
  67.9 4.4 collective-permute-start.2
  67.9 4.4 collective-permute-start.3
  72.3 4.4 collective-permute-start.4
  72.3 4.6 collective-permute-start.5
  76.7 4.4 collective-permute-start.6
  76.8 4.4 collective-permute-start.7
  81.1 4.4 collective-permute-start.8
  81.2 4.4 collective-permute-start.9
  85.5 5.0 collective-permute-start.10
  85.6 4.8 collective-permute-start.11
  90.4 5.6 collective-permute-start.12
  90.4 6.3 collective-permute-start.13
  96.1 5.6 collective-permute-start.14
  102.3 5.7 copy-start.5
  107.9 228.1 %copy-start.4 = (bf16[384,32]{0,1:T(8,128)(2,1)S(1)}, bf16[384,32]{0,1:T(8,128)(2,1)}, u32[]{:S(2)}) copy-start(bf16[384,32]{0,1:T(8,128)(2,1)} %param.9) | copy-start | bytes 73732
  108.0 327.1 %all-gather.5.cloned.1.call-start = ((), (), s32[]{:S(2)}) async-start(), calls=%async_computation.5 | async-start | bytes 2433024 | tf_op jit(solution)/shard_map/all_gather | solution.py:81
  336.9 19.7 %copy-start.7 = (bf16[1024]{0:T(1024)(128)(2,1)S(1)}, bf16[1024]{0:T(1024)(128)(2,1)}, u32[]{:S(2)}) copy-start(bf16[1024]{0:T(1024)(128)(2,1)} %param.13) | copy-start | bytes 6148
  356.4 315.8 %reduce-scatter.5.cloned.1.call-start = ((), (), s32[]{:S(2)}) async-start(), calls=%async_computation.6 | async-start | bytes 540672 | tf_op jit(solution)/shard_map/reduce_scatter | solution.py:103
  435.0 2.4 copy-start.1
  440.9 1.6 copy-start.8
  448.0 3.3 copy-start.2
Sparse Core Ops, SparseCore 0:
  9.5 45.9 all-gather.2
  108.1 227.8 reduce-scatter.2
  356.5 78.4 all-gather.4
  452.7 219.4 reduce-scatter.4
